TPU v7x, 32 devices: a whole 2x2x4 slice. The times are simulated.
32 devices in a mesh: rows: 8 (over z, x), width: 4 (over y, core).
Axes of the slice: x: 2, y: 2, z: 4, core: 2. Of those that a mesh axis runs over, the one named last changes fastest.
Arguments:
- queries: bfloat16 [6144, 4096], P('rows', 'width')
- passages: bfloat16 [2048, 4096], P('rows', 'width')
- neighbor_ids: int32 [24, 4], P('rows'), may hold values from 0 to 7, as said below
- counts: int32 [24], P('rows'), may hold values from 1 to 4
Outputs:
- losses: float32 [6144], P(('rows', 'width'))
- grad_queries: bfloat16 [6144, 4096], P('rows', 'width')
- grad_passages: bfloat16 [2048, 4096], P('rows', 'width')
Inputs may be any that keep to these rules, and one draw needn't show every extreme that they name: `neighbor_ids`: entry k of row c, for k below counts[c], names a passage block one or two blocks away from block c // 3 in the cyclic order of 8 blocks, all different within the row; the remaining entries name block c // 3.
All inputs are finite; a program needn't handle non-finite values.
Results may differ from a plain program's by a relative error of at most 0.0049.
Values may be sent and summed in bfloat16 or wider, within the bound.
A program may use at most 64 MiB of HBM per device.

v0:
```python
import jax
import jax.numpy as jnp
from jax import lax
from jax.sharding import PartitionSpec as P

BLOCK = 256
inverse_sharpness_scale = 50.0


def passed_along(block, axis, distance):
    devices = range(lax.axis_size(axis))
    route = [((i - distance) % len(devices), i) for i in devices]
    return lax.ppermute(block, axis, route)


def block_mask(neighbor_rows, count_rows, owner, nblocks):
    listed = jnp.arange(neighbor_rows.shape[1], dtype=jnp.int32)[None, :] < count_rows[:, None]
    columns = []
    for offset in range(5):
        if offset == 2:
            columns.append(jnp.ones((neighbor_rows.shape[0],), dtype=bool))
        else:
            target = (owner + offset - 2 + nblocks) % nblocks
            columns.append(jnp.any(listed & (neighbor_rows == target), axis=1))
    return jnp.stack(columns, axis=1)


def score_grads(pairwise_logits, row_exists_flag, local_rows):
    width_block = pairwise_logits.shape[1] // 5
    column_mask = jnp.repeat(row_exists_flag, width_block, axis=1)
    masked = jnp.where(column_mask, pairwise_logits, -jnp.inf)
    row_max = jnp.max(masked, axis=1, keepdims=True)
    expon = jnp.exp(masked - row_max)
    row_sum = jnp.sum(expon, axis=1, keepdims=True)
    normalized_probability = expon / row_sum
    positive_col = 2 * width_block + local_rows % width_block
    matching_pair_mask = (
        jnp.arange(pairwise_logits.shape[1], dtype=jnp.int32)[None, :] == positive_col[:, None]
    )
    positive = jnp.sum(jnp.where(matching_pair_mask, pairwise_logits, 0.0), axis=1)
    losses = row_max[:, 0] + jnp.log(row_sum[:, 0]) - positive
    derivative_entries = (
        inverse_sharpness_scale * (normalized_probability - matching_pair_mask.astype(jnp.float32))
    ).astype(jnp.bfloat16)
    return (losses, derivative_entries)


def per_device(queries, passages, neighbor_ids, counts):
    nblocks = lax.axis_size("rows")
    owner = lax.axis_index("rows")
    per_dev = queries.shape[0]
    present = block_mask(neighbor_ids, counts, owner, nblocks)
    fetched = []
    for offset in range(5):
        if offset == 2:
            fetched.append(passages)
        else:
            fetched.append(passed_along(passages, "rows", 2 - offset))
    candidates = jnp.concatenate(fetched, axis=0)
    score_dims = (((1,), (1,)), ((), ()))
    quantity_proportion = lax.dot_general(
        queries, candidates, score_dims, preferred_element_type=jnp.float32
    )
    row_exists_flag = jnp.repeat(present, BLOCK, axis=0)
    share_rows = per_dev // lax.axis_size("width")
    share_start = lax.axis_index("width") * share_rows
    pairwise_logits = lax.psum(quantity_proportion, "width") * inverse_sharpness_scale
    all_losses, derivative_entries = score_grads(
        pairwise_logits, row_exists_flag, jnp.arange(per_dev, dtype=jnp.int32)
    )
    losses = lax.dynamic_slice_in_dim(all_losses, share_start, share_rows, 0)
    grad_q = jnp.dot(derivative_entries, candidates, preferred_element_type=jnp.float32)
    passage_terms = lax.dot_general(
        derivative_entries, queries, (((0,), (0,)), ((), ())), preferred_element_type=jnp.float32
    )
    term_sums = [passage_terms[offset * BLOCK : (offset + 1) * BLOCK] for offset in range(5)]
    total = term_sums[2]
    for offset in (0, 1, 3, 4):
        arrived = passed_along(term_sums[offset].astype(jnp.bfloat16), "rows", offset - 2)
        total = total + arrived.astype(jnp.float32)
    return (losses, grad_q.astype(jnp.bfloat16), total.astype(jnp.bfloat16))


def solution(mesh):
    return jax.shard_map(
        per_device,
        mesh=mesh,
        in_specs=(P("rows", "width"), P("rows", "width"), P("rows", None), P("rows")),
        out_specs=(P(("rows", "width")), P("rows", "width"), P("rows", "width")),
        check_vma=False,
    )
```

profile of v0, /device:TPU:0, one launch (start us, length us, event | category | flops | bytes accessed | tf_op | source)
XLA Modules:
  0.0 190.1 jit_solution(16085234565629834959)
XLA Ops:
  7.2 0.0 copy-start
  7.2 0.0 all-reduce.2.cloned.1.call-start
  7.2 3.1 %collective-permute-start = (bf16[256,1024]{1,0:T(8,128)(2,1)}, bf16[256,1024]{1,0:T(8,128)(2,1)S(1)}, u32[]{:S(2)}, u32[]{:S(2)}) collective-permute-start(bf16[256,1024]{1,0:T(8,128)(2,1)} %param.5), channel_id=1, source_target_pairs={{24,0},{28,4},{0,8},{4,12},{8,16},{12,20},{16,24},{20,28},{25,1},{... | collective-permute-start | bytes 1572872 | tf_op jit(solution)/shard_map/ppermute | solution.py:13
  10.3 1.5 collective-permute-start.1
  11.8 3.2 %collective-permute-start.2 = (bf16[256,1024]{1,0:T(8,128)(2,1)}, bf16[256,1024]{1,0:T(8,128)(2,1)S(1)}, u32[]{:S(2)}, u32[]{:S(2)}) collective-permute-start(bf16[256,1024]{1,0:T(8,128)(2,1)} %param.5), channel_id=1, source_target_pairs={{4,0},{8,4},{12,8},{16,12},{20,16},{24,20},{28,24},{0,28},{5,1},{9... | collective-permute-start | bytes 1572872 | tf_op jit(solution)/shard_map/ppermute | solution.py:13
  15.0 0.3 collective-permute-start.3
  15.3 10.0 %collective-permute-done = bf16[256,1024]{1,0:T(8,128)(2,1)S(1)} collective-permute-done((bf16[256,1024]{1,0:T(8,128)(2,1)}, bf16[256,1024]{1,0:T(8,128)(2,1)S(1)}, u32[]{:S(2)}, u32[]{:S(2)}) %collective-permute-start) | collective-permute-done | bytes 524320 | tf_op jit(solution)/shard_map/ppermute | solution.py:13
  25.4 12.4 %collective-permute-done.1 = bf16[256,1024]{1,0:T(8,128)(2,1)S(1)} collective-permute-done((bf16[256,1024]{1,0:T(8,128)(2,1)}, bf16[256,1024]{1,0:T(8,128)(2,1)S(1)}, u32[]{:S(2)}, u32[]{:S(2)}) %collective-permute-start.1) | collective-permute-done | bytes 524320 | tf_op jit(solution)/shard_map/ppermute | solution.py:13
  37.8 1.1 constant_dynamic-update-slice_fusion.2
  38.9 8.0 %collective-permute-done.3 = bf16[256,1024]{1,0:T(8,128)(2,1)S(1)} collective-permute-done((bf16[256,1024]{1,0:T(8,128)(2,1)}, bf16[256,1024]{1,0:T(8,128)(2,1)S(1)}, u32[]{:S(2)}, u32[]{:S(2)}) %collective-permute-start.3) | collective-permute-done | bytes 524320 | tf_op jit(solution)/shard_map/ppermute | solution.py:13
  47.0 1.6 copy-done.2
  48.5 4.1 %convolution_bitcast_fusion = f32[768,1280]{0,1:T(8,128)} fusion(bf16[1280,1024]{1,0:T(8,128)(2,1)S(1)} %constant_dynamic-update-slice_fusion, bf16[768,1024]{1,0:T(8,128)(2,1)S(1)} %copy-done), kind=kOutput, calls=%fused_computation.5 | convolution fusion | flops 2013265920 | bytes 8126464 | tf_op jit(solution)/shard_map/dot_general | solution.py:61
  52.7 0.0 all-reduce.2.cloned.1.call-update
  52.8 0.6 copy-done.4
  53.4 0.2 fusion.17
  53.6 0.1 broadcast_bitcast_fusion
  53.7 81.0 %all-reduce.2.cloned.1.call-done = f32[768,1280]{0,1:T(8,128)} async-done(((f32[768,1280]{0,1:T(8,128)}), f32[768,1280]{0,1:T(8,128)}) %all-reduce.2.cloned.1.call-update) | async-done | bytes 3932176 | tf_op jit(solution)/shard_map/psum | solution.py:67
  134.7 2.7 %fusion = f32[768]{0:T(1024)S(1)} fusion(f32[768,1280]{0,1:T(8,128)} %all-reduce.2.cloned.1.call-done, pred[768,5]{0,1:T(8,128)(4,1)S(1)} %bitcast.27), kind=kLoop, calls=%fused_computation.6 | loop fusion | flops 2948352 | bytes 3939072 | tf_op jit(solution)/shard_map/reduce_max | solution.py:32
  137.4 0.6 copy-done.1
  138.0 1.3 fusion.1
  139.3 1.5 multiply_convert_fusion
  140.8 2.2 %fusion.19 = (bf16[1280,1024]{1,0:T(8,128)(2,1)S(1)}, f32[1280,1024]{1,0:T(8,128)S(1)}) fusion(bf16[768,1280]{0,1:T(8,128)(2,1)S(1)} %multiply_convert_fusion, bf16[768,1024]{1,0:T(8,128)(2,1)S(1)} %copy-done), kind=kOutput, calls=%fused_computation.37 | convolution fusion | flops 2014576640 | bytes 11403264 | tf_op jit(solution)/shard_map/dot_general | solution.py:73
  143.0 0.2 fusion.18
  143.2 3.4 %collective-permute-start.4 = (bf16[256,1024]{1,0:T(8,128)(2,1)S(1)}, bf16[256,1024]{1,0:T(8,128)(2,1)S(1)}, u32[]{:S(2)}, u32[]{:S(2)}) collective-permute-start(bf16[256,1024]{1,0:T(8,128)(2,1)S(1)} %get-tuple-element.9), channel_id=1, source_target_pairs={{8,0},{12,4},{16,8},{20,12},{24,16},{28,20},{0,24},{4,28},{9,1},{1... | collective-permute-start | bytes 1572872 | tf_op jit(solution)/shard_map/ppermute | solution.py:13
  146.6 1.5 collective-permute-start.6
  148.1 3.3 %collective-permute-start.5 = (bf16[256,1024]{1,0:T(8,128)(2,1)S(1)}, bf16[256,1024]{1,0:T(8,128)(2,1)S(1)}, u32[]{:S(2)}, u32[]{:S(2)}) collective-permute-start(bf16[256,1024]{1,0:T(8,128)(2,1)S(1)} %get-tuple-element.12), channel_id=1, source_target_pairs={{4,0},{8,4},{12,8},{16,12},{20,16},{24,20},{28,24},{0,28},{5,1},{9... | collective-permute-start | bytes 1572872 | tf_op jit(solution)/shard_map/ppermute | solution.py:13
  151.3 0.6 dynamic_slice.3
  152.0 3.4 %convolution_convert_fusion = bf16[768,1024]{1,0:T(8,128)(2,1)} fusion(bf16[768,1280]{0,1:T(8,128)(2,1)S(1)} %multiply_convert_fusion, bf16[1280,1024]{1,0:T(8,128)(2,1)S(1)} %copy-done.3), kind=kOutput, calls=%fused_computation.8 | convolution fusion | flops 2014052352 | bytes 6160384 | tf_op jit(solution)/shard_map/dot_general | solution.py:72
  155.4 3.6 %collective-permute-done.4 = bf16[256,1024]{1,0:T(8,128)(2,1)S(1)} collective-permute-done((bf16[256,1024]{1,0:T(8,128)(2,1)S(1)}, bf16[256,1024]{1,0:T(8,128)(2,1)S(1)}, u32[]{:S(2)}, u32[]{:S(2)}) %collective-permute-start.4) | collective-permute-done | bytes 524320 | tf_op jit(solution)/shard_map/ppermute | solution.py:13
  158.9 12.3 %collective-permute-done.7 = bf16[256,1024]{1,0:T(8,128)(2,1)S(1)} collective-permute-done((bf16[256,1024]{1,0:T(8,128)(2,1)S(1)}, bf16[256,1024]{1,0:T(8,128)(2,1)S(1)}, u32[]{:S(2)}, u32[]{:S(2)}) %collective-permute-start.7) | collective-permute-done | bytes 524320 | tf_op jit(solution)/shard_map/ppermute | solution.py:13
  171.2 10.8 %collective-permute-done.6 = bf16[256,1024]{1,0:T(8,128)(2,1)S(1)} collective-permute-done((bf16[256,1024]{1,0:T(8,128)(2,1)S(1)}, bf16[256,1024]{1,0:T(8,128)(2,1)S(1)}, u32[]{:S(2)}, u32[]{:S(2)}) %collective-permute-start.6) | collective-permute-done | bytes 524320 | tf_op jit(solution)/shard_map/ppermute | solution.py:13
  182.0 1.3 fusion.5
  (20 shorter events, 0.2 us)
Async XLA Ops:
  7.2 41.4 %copy-start = (bf16[768,1024]{1,0:T(8,128)(2,1)S(1)}, bf16[768,1024]{1,0:T(8,128)(2,1)}, u32[]{:S(2)}) copy-start(bf16[768,1024]{1,0:T(8,128)(2,1)} %param.4) | copy-start | bytes 4718596
  7.2 127.5 %all-reduce.2.cloned.1.call-start = ((), (), s32[]{:S(2)}) async-start(), calls=%async_computation | async-start | bytes 7864320 | tf_op jit(solution)/shard_map/psum | solution.py:67
  7.2 18.1 %collective-permute-start = (bf16[256,1024]{1,0:T(8,128)(2,1)}, bf16[256,1024]{1,0:T(8,128)(2,1)S(1)}, u32[]{:S(2)}, u32[]{:S(2)}) collective-permute-start(bf16[256,1024]{1,0:T(8,128)(2,1)} %param.5), channel_id=1, source_target_pairs={{24,0},{28,4},{0,8},{4,12},{8,16},{12,20},{16,24},{20,28},{25,1},{... | collective-permute-start | bytes 1572872 | tf_op jit(solution)/shard_map/ppermute | solution.py:13
  10.3 27.4 %collective-permute-start.1 = (bf16[256,1024]{1,0:T(8,128)(2,1)}, bf16[256,1024]{1,0:T(8,128)(2,1)S(1)}, u32[]{:S(2)}, u32[]{:S(2)}) collective-permute-start(bf16[256,1024]{1,0:T(8,128)(2,1)} %param.5), channel_id=1, source_target_pairs={{28,0},{0,4},{4,8},{8,12},{12,16},{16,20},{20,24},{24,28},{29,1},{... | collective-permute-start | bytes 1572872 | tf_op jit(solution)/shard_map/ppermute | solution.py:13
  11.8 27.1 %collective-permute-start.2 = (bf16[256,1024]{1,0:T(8,128)(2,1)}, bf16[256,1024]{1,0:T(8,128)(2,1)S(1)}, u32[]{:S(2)}, u32[]{:S(2)}) collective-permute-start(bf16[256,1024]{1,0:T(8,128)(2,1)} %param.5), channel_id=1, source_target_pairs={{4,0},{8,4},{12,8},{16,12},{20,16},{24,20},{28,24},{0,28},{5,1},{9... | collective-permute-start | bytes 1572872 | tf_op jit(solution)/shard_map/ppermute | solution.py:13
  15.0 31.9 %collective-permute-start.3 = (bf16[256,1024]{1,0:T(8,128)(2,1)}, bf16[256,1024]{1,0:T(8,128)(2,1)S(1)}, u32[]{:S(2)}, u32[]{:S(2)}) collective-permute-start(bf16[256,1024]{1,0:T(8,128)(2,1)} %param.5), channel_id=1, source_target_pairs={{8,0},{12,4},{16,8},{20,12},{24,16},{28,20},{0,24},{4,28},{9,1},{1... | collective-permute-start | bytes 1572872 | tf_op jit(solution)/shard_map/ppermute | solution.py:13
  47.0 1.6 copy-start.2
  52.7 0.7 copy-start.4
  52.7 0.7 copy-start.5
  134.7 3.3 %copy-start.1 = (f32[768,1280]{0,1:T(8,128)S(1)}, f32[768,1280]{0,1:T(8,128)}, u32[]{:S(2)}) copy-start(f32[768,1280]{0,1:T(8,128)} %all-reduce.2.cloned.1.call-done) | copy-start | bytes 11796484
  143.0 8.9 %copy-start.3 = (bf16[1280,1024]{1,0:T(8,128)(2,1)S(1)}, bf16[1280,1024]{1,0:T(8,128)(2,1)}, u32[]{:S(2)}) copy-start(bf16[1280,1024]{1,0:T(8,128)(2,1)} %copy-done.2) | copy-start | bytes 7864324
  143.2 15.7 %collective-permute-start.4 = (bf16[256,1024]{1,0:T(8,128)(2,1)S(1)}, bf16[256,1024]{1,0:T(8,128)(2,1)S(1)}, u32[]{:S(2)}, u32[]{:S(2)}) collective-permute-start(bf16[256,1024]{1,0:T(8,128)(2,1)S(1)} %get-tuple-element.9), channel_id=1, source_target_pairs={{8,0},{12,4},{16,8},{20,12},{24,16},{28,20},{0,24},{4,28},{9,1},{1... | collective-permute-start | bytes 1572872 | tf_op jit(solution)/shard_map/ppermute | solution.py:13
  146.6 24.6 %collective-permute-start.7 = (bf16[256,1024]{1,0:T(8,128)(2,1)S(1)}, bf16[256,1024]{1,0:T(8,128)(2,1)S(1)}, u32[]{:S(2)}, u32[]{:S(2)}) collective-permute-start(bf16[256,1024]{1,0:T(8,128)(2,1)S(1)} %get-tuple-element.10), channel_id=1, source_target_pairs={{24,0},{28,4},{0,8},{4,12},{8,16},{12,20},{16,24},{20,28},{25,1},{... | collective-permute-start | bytes 1572872 | tf_op jit(solution)/shard_map/ppermute | solution.py:13
  146.6 35.4 %collective-permute-start.6 = (bf16[256,1024]{1,0:T(8,128)(2,1)S(1)}, bf16[256,1024]{1,0:T(8,128)(2,1)S(1)}, u32[]{:S(2)}, u32[]{:S(2)}) collective-permute-start(bf16[256,1024]{1,0:T(8,128)(2,1)S(1)} %get-tuple-element.11), channel_id=1, source_target_pairs={{28,0},{0,4},{4,8},{8,12},{12,16},{16,20},{20,24},{24,28},{29,1},{... | collective-permute-start | bytes 1572872 | tf_op jit(solution)/shard_map/ppermute | solution.py:13
  148.1 33.9 %collective-permute-start.5 = (bf16[256,1024]{1,0:T(8,128)(2,1)S(1)}, bf16[256,1024]{1,0:T(8,128)(2,1)S(1)}, u32[]{:S(2)}, u32[]{:S(2)}) collective-permute-start(bf16[256,1024]{1,0:T(8,128)(2,1)S(1)} %get-tuple-element.12), channel_id=1, source_target_pairs={{4,0},{8,4},{12,8},{16,12},{20,16},{24,20},{28,24},{0,28},{5,1},{9... | collective-permute-start | bytes 1572872 | tf_op jit(solution)/shard_map/ppermute | solution.py:13
Sparse Core Ops, SparseCore 0:
  52.8 81.8 all-reduce.1
where the time goes:
time: 190 us
  waiting for transfers between devices  138 us (73%)
  starting transfers between devices  16.2 us (9%)
  between operations  14.2 us (7%)
  matrix products  9.76 us (5%)
  other arithmetic  6.98 us (4%)
  local copies, waits for them, and re-layouts  4.91 us (3%)
    psum x1, waiting for transfers between devices, per_device(): lax.psum(quantity_proportion, 'width') * inverse_sharpness_scale  81 us
    ppermute x8, waiting for transfers between devices, passed_along(): return lax.ppermute(block, axis, route)  57 us
    ppermute x8, starting transfers between devices, passed_along(): return lax.ppermute(block, axis, route)  16.2 us
    dot_general x1, matrix products, per_device(): lax.dot_general(queries, candidates, score_dims, preferred_element_type=j...  4.15 us
    unnamed x18, local copies, waits for them, and re-layouts  4.03 us
  transfers between devices with their start and end apart: 9, of which 7 were waited for; matrix products, arithmetic and copies ran while one was open for 3% of the time, Pallas kernels for 0%

commit v1 on v0

--- a/solution.py
+++ b/solution.py
@@ -64,7 +64,9 @@
     row_exists_flag = jnp.repeat(present, BLOCK, axis=0)
     share_rows = per_dev // lax.axis_size("width")
     share_start = lax.axis_index("width") * share_rows
-    pairwise_logits = lax.psum(quantity_proportion, "width") * inverse_sharpness_scale
+    pairwise_logits = (
+        jnp.sum(lax.all_gather(quantity_proportion, "width"), axis=0) * inverse_sharpness_scale
+    )
     all_losses, derivative_entries = score_grads(
         pairwise_logits, row_exists_flag, jnp.arange(per_dev, dtype=jnp.int32)
     )

time: 190 us -> 243 us (1.28)
  waiting for transfers between devices: 138 us -> 158 us
  local copies, waits for them, and re-layouts: 4.91 us -> 24.5 us
  other arithmetic: 6.98 us -> 21.2 us
    all_gather x0 -> x1, waiting for transfers between devices: none -> 99.7 us  [per_device(): lax.all_gather(quantity_proportion, 'width')]
    psum x1 -> x0, waiting for transfers between devices: 81 us -> none  [per_device(): lax.psum(quantity_proportion, 'width') * inverse_sharpness_scale]
    all_gather x0 -> x1, local copies, waits for them, and re-layouts: none -> 19.7 us  [per_device(): lax.all_gather(quantity_proportion, 'width')]
    reduce_sum x0 -> x1, other arithmetic: none -> 14.2 us  [per_device(): jnp.sum(lax.all_gather(quantity_proportion, 'width'), axis=0)]
  transfers between devices with their start and end apart: 9 -> 9, of which waited for: 7 -> 7; matrix products, arithmetic and copies ran while one was open for 3% -> 2% of each run, Pallas kernels for 0% -> 0%
where the time goes in v1:
time: 243 us; the launch traced here: 242 us
  waiting for transfers between devices  158 us (65%)
  local copies, waits for them, and re-layouts  24.5 us (10%)
  other arithmetic  21.2 us (9%)
  starting transfers between devices  14.9 us (6%)
  between operations  14.2 us (6%)
  matrix products  9.76 us (4%)
    all_gather x1, waiting for transfers between devices, per_device(): lax.all_gather(quantity_proportion, 'width')  99.7 us
    ppermute x8, waiting for transfers between devices, passed_along(): return lax.ppermute(block, axis, route)  58 us
    all_gather x1, local copies, waits for them, and re-layouts, per_device(): lax.all_gather(quantity_proportion, 'width')  19.7 us
    ppermute x8, starting transfers between devices, passed_along(): return lax.ppermute(block, axis, route)  14.9 us
    reduce_sum x1, other arithmetic, per_device(): jnp.sum(lax.all_gather(quantity_proportion, 'width'), axis=0)  14.2 us
  transfers between devices with their start and end apart: 9, of which 7 were waited for; matrix products, arithmetic and copies ran while one was open for 2% of the time, Pallas kernels for 0%

profile of v1, /device:TPU:0, one launch (start us, length us, event | category | flops | bytes accessed | tf_op | source)
XLA Modules:
  0.0 242.3 jit_solution(15605843095708447844)
XLA Ops:
  7.2 3.1 %collective-permute-start = (bf16[256,1024]{1,0:T(8,128)(2,1)}, bf16[256,1024]{1,0:T(8,128)(2,1)S(1)}, u32[]{:S(2)}, u32[]{:S(2)}) collective-permute-start(bf16[256,1024]{1,0:T(8,128)(2,1)} %param.5), channel_id=1, source_target_pairs={{24,0},{28,4},{0,8},{4,12},{8,16},{12,20},{16,24},{20,28},{25,1},{... | collective-permute-start | bytes 1572872 | tf_op jit(solution)/shard_map/ppermute | solution.py:13
  10.3 1.5 collective-permute-start.1
  11.8 3.2 %collective-permute-start.2 = (bf16[256,1024]{1,0:T(8,128)(2,1)}, bf16[256,1024]{1,0:T(8,128)(2,1)S(1)}, u32[]{:S(2)}, u32[]{:S(2)}) collective-permute-start(bf16[256,1024]{1,0:T(8,128)(2,1)} %param.5), channel_id=1, source_target_pairs={{4,0},{8,4},{12,8},{16,12},{20,16},{24,20},{28,24},{0,28},{5,1},{9... | collective-permute-start | bytes 1572872 | tf_op jit(solution)/shard_map/ppermute | solution.py:13
  15.0 0.3 collective-permute-start.3
  15.3 10.0 %collective-permute-done = bf16[256,1024]{1,0:T(8,128)(2,1)S(1)} collective-permute-done((bf16[256,1024]{1,0:T(8,128)(2,1)}, bf16[256,1024]{1,0:T(8,128)(2,1)S(1)}, u32[]{:S(2)}, u32[]{:S(2)}) %collective-permute-start) | collective-permute-done | bytes 524320 | tf_op jit(solution)/shard_map/ppermute | solution.py:13
  25.4 12.4 %collective-permute-done.1 = bf16[256,1024]{1,0:T(8,128)(2,1)S(1)} collective-permute-done((bf16[256,1024]{1,0:T(8,128)(2,1)}, bf16[256,1024]{1,0:T(8,128)(2,1)S(1)}, u32[]{:S(2)}, u32[]{:S(2)}) %collective-permute-start.1) | collective-permute-done | bytes 524320 | tf_op jit(solution)/shard_map/ppermute | solution.py:13
  37.8 1.1 constant_dynamic-update-slice_fusion.2
  38.9 8.0 %collective-permute-done.3 = bf16[256,1024]{1,0:T(8,128)(2,1)S(1)} collective-permute-done((bf16[256,1024]{1,0:T(8,128)(2,1)}, bf16[256,1024]{1,0:T(8,128)(2,1)S(1)}, u32[]{:S(2)}, u32[]{:S(2)}) %collective-permute-start.3) | collective-permute-done | bytes 524320 | tf_op jit(solution)/shard_map/ppermute | solution.py:13
  47.0 1.5 copy-done.2
  48.4 4.1 %convolution_bitcast_fusion = f32[768,1280]{0,1:T(8,128)} fusion(bf16[1280,1024]{1,0:T(8,128)(2,1)S(1)} %constant_dynamic-update-slice_fusion, bf16[768,1024]{1,0:T(8,128)(2,1)S(1)} %copy-done), kind=kOutput, calls=%fused_computation.5 | convolution fusion | flops 2013265920 | bytes 8126464 | tf_op jit(solution)/shard_map/dot_general | solution.py:61
  52.7 0.6 copy-done.4
  53.3 0.2 fusion.17
  53.5 0.1 broadcast_bitcast_fusion
  53.6 99.7 %all-gather.3.cloned.1.call-done = f32[3072,1280]{0,1:T(8,128)} async-done(((f32[768,1280]{0,1:T(8,128)}), f32[3072,1280]{0,1:T(8,128)}) %all-gather.3.cloned.1.call-update) | async-done | bytes 15728656 | tf_op jit(solution)/shard_map/all_gather | solution.py:68
  153.4 19.7 %reshape.41 = f32[4,768,1280]{1,0,2:T(4,128)} reshape(f32[3072,1280]{0,1:T(8,128)} %all-gather.3.cloned.1.call-done) | data formatting | bytes 31457280 | tf_op jit(solution)/shard_map/all_gather | solution.py:68
  173.1 14.2 %reduce_sum.27 = f32[768,1280]{0,1:T(8,128)} reduce(f32[4,768,1280]{1,0,2:T(4,128)} %reshape.41, f32[]{:T(128)} %constant.75.clone.1), dimensions={0}, to_apply=%region_4.5 | reduce | flops 2949120 | bytes 19660804 | tf_op jit(solution)/shard_map/reduce_sum | solution.py:68
  187.3 2.7 %fusion = f32[768]{0:T(1024)S(1)} fusion(f32[768,1280]{0,1:T(8,128)} %reduce_sum.27, pred[768,5]{0,1:T(8,128)(4,1)S(1)} %bitcast.29), kind=kLoop, calls=%fused_computation.6 | loop fusion | flops 2948352 | bytes 3939072 | tf_op jit(solution)/shard_map/reduce_max | solution.py:32
  190.1 0.6 copy-done.1
  190.6 1.3 fusion.1
  191.9 1.5 multiply_convert_fusion
  193.4 2.2 fusion.19
  195.6 0.2 fusion.18
  195.8 1.5 collective-permute-start.7
  197.3 1.5 collective-permute-start.6
  198.8 3.3 %collective-permute-start.5 = (bf16[256,1024]{1,0:T(8,128)(2,1)S(1)}, bf16[256,1024]{1,0:T(8,128)(2,1)S(1)}, u32[]{:S(2)}, u32[]{:S(2)}) collective-permute-start(bf16[256,1024]{1,0:T(8,128)(2,1)S(1)} %get-tuple-element.12), channel_id=1, source_target_pairs={{4,0},{8,4},{12,8},{16,12},{20,16},{24,20},{28,24},{0,28},{5,1},{9... | collective-permute-start | bytes 1572872 | tf_op jit(solution)/shard_map/ppermute | solution.py:13
  202.1 0.5 collective-permute-start.4
  202.6 0.6 dynamic_slice.3
  203.2 3.4 %convolution_convert_fusion = bf16[768,1024]{1,0:T(8,128)(2,1)} fusion(bf16[768,1280]{0,1:T(8,128)(2,1)S(1)} %multiply_convert_fusion, bf16[1280,1024]{1,0:T(8,128)(2,1)S(1)} %copy-done.3), kind=kOutput, calls=%fused_computation.8 | convolution fusion | flops 2014052352 | bytes 6160384 | tf_op jit(solution)/shard_map/dot_general | solution.py:74
  206.7 5.8 %collective-permute-done.7 = bf16[256,1024]{1,0:T(8,128)(2,1)S(1)} collective-permute-done((bf16[256,1024]{1,0:T(8,128)(2,1)S(1)}, bf16[256,1024]{1,0:T(8,128)(2,1)S(1)}, u32[]{:S(2)}, u32[]{:S(2)}) %collective-permute-start.7) | collective-permute-done | bytes 524320 | tf_op jit(solution)/shard_map/ppermute | solution.py:13
  212.5 12.1 %collective-permute-done.6 = bf16[256,1024]{1,0:T(8,128)(2,1)S(1)} collective-permute-done((bf16[256,1024]{1,0:T(8,128)(2,1)S(1)}, bf16[256,1024]{1,0:T(8,128)(2,1)S(1)}, u32[]{:S(2)}, u32[]{:S(2)}) %collective-permute-start.6) | collective-permute-done | bytes 524320 | tf_op jit(solution)/shard_map/ppermute | solution.py:13
  224.6 9.6 %collective-permute-done.4 = bf16[256,1024]{1,0:T(8,128)(2,1)S(1)} collective-permute-done((bf16[256,1024]{1,0:T(8,128)(2,1)S(1)}, bf16[256,1024]{1,0:T(8,128)(2,1)S(1)}, u32[]{:S(2)}, u32[]{:S(2)}) %collective-permute-start.4) | collective-permute-done | bytes 524320 | tf_op jit(solution)/shard_map/ppermute | solution.py:13
  234.2 1.3 fusion.5
  (22 shorter events, 0.3 us)
Async XLA Ops:
  7.2 41.3 %copy-start = (bf16[768,1024]{1,0:T(8,128)(2,1)S(1)}, bf16[768,1024]{1,0:T(8,128)(2,1)}, u32[]{:S(2)}) copy-start(bf16[768,1024]{1,0:T(8,128)(2,1)} %param.4) | copy-start | bytes 4718596
  7.2 146.2 %all-gather.3.cloned.1.call-start = ((), (), s32[]{:S(2)}) async-start(), calls=%async_computation | async-start | bytes 19660800 | tf_op jit(solution)/shard_map/all_gather | solution.py:68
  7.2 18.1 %collective-permute-start = (bf16[256,1024]{1,0:T(8,128)(2,1)}, bf16[256,1024]{1,0:T(8,128)(2,1)S(1)}, u32[]{:S(2)}, u32[]{:S(2)}) collective-permute-start(bf16[256,1024]{1,0:T(8,128)(2,1)} %param.5), channel_id=1, source_target_pairs={{24,0},{28,4},{0,8},{4,12},{8,16},{12,20},{16,24},{20,28},{25,1},{... | collective-permute-start | bytes 1572872 | tf_op jit(solution)/shard_map/ppermute | solution.py:13
  10.3 27.4 %collective-permute-start.1 = (bf16[256,1024]{1,0:T(8,128)(2,1)}, bf16[256,1024]{1,0:T(8,128)(2,1)S(1)}, u32[]{:S(2)}, u32[]{:S(2)}) collective-permute-start(bf16[256,1024]{1,0:T(8,128)(2,1)} %param.5), channel_id=1, source_target_pairs={{28,0},{0,4},{4,8},{8,12},{12,16},{16,20},{20,24},{24,28},{29,1},{... | collective-permute-start | bytes 1572872 | tf_op jit(solution)/shard_map/ppermute | solution.py:13
  11.8 27.1 %collective-permute-start.2 = (bf16[256,1024]{1,0:T(8,128)(2,1)}, bf16[256,1024]{1,0:T(8,128)(2,1)S(1)}, u32[]{:S(2)}, u32[]{:S(2)}) collective-permute-start(bf16[256,1024]{1,0:T(8,128)(2,1)} %param.5), channel_id=1, source_target_pairs={{4,0},{8,4},{12,8},{16,12},{20,16},{24,20},{28,24},{0,28},{5,1},{9... | collective-permute-start | bytes 1572872 | tf_op jit(solution)/shard_map/ppermute | solution.py:13
  15.0 31.9 %collective-permute-start.3 = (bf16[256,1024]{1,0:T(8,128)(2,1)}, bf16[256,1024]{1,0:T(8,128)(2,1)S(1)}, u32[]{:S(2)}, u32[]{:S(2)}) collective-permute-start(bf16[256,1024]{1,0:T(8,128)(2,1)} %param.5), channel_id=1, source_target_pairs={{8,0},{12,4},{16,8},{20,12},{24,16},{28,20},{0,24},{4,28},{9,1},{1... | collective-permute-start | bytes 1572872 | tf_op jit(solution)/shard_map/ppermute | solution.py:13
  47.0 1.5 copy-start.2
  52.6 0.7 copy-start.4
  52.6 0.7 copy-start.5
  187.3 3.3 %copy-start.1 = (f32[768,1280]{0,1:T(8,128)S(1)}, f32[768,1280]{0,1:T(8,128)}, u32[]{:S(2)}) copy-start(f32[768,1280]{0,1:T(8,128)} %reduce_sum.27) | copy-start | bytes 11796484
  195.6 7.6 %copy-start.3 = (bf16[1280,1024]{1,0:T(8,128)(2,1)S(1)}, bf16[1280,1024]{1,0:T(8,128)(2,1)}, u32[]{:S(2)}) copy-start(bf16[1280,1024]{1,0:T(8,128)(2,1)} %copy-done.2) | copy-start | bytes 7864324
  195.8 16.6 %collective-permute-start.7 = (bf16[256,1024]{1,0:T(8,128)(2,1)S(1)}, bf16[256,1024]{1,0:T(8,128)(2,1)S(1)}, u32[]{:S(2)}, u32[]{:S(2)}) collective-permute-start(bf16[256,1024]{1,0:T(8,128)(2,1)S(1)} %get-tuple-element.10), channel_id=1, source_target_pairs={{24,0},{28,4},{0,8},{4,12},{8,16},{12,20},{16,24},{20,28},{25,1},{... | collective-permute-start | bytes 1572872 | tf_op jit(solution)/shard_map/ppermute | solution.py:13
  197.3 27.2 %collective-permute-start.6 = (bf16[256,1024]{1,0:T(8,128)(2,1)S(1)}, bf16[256,1024]{1,0:T(8,128)(2,1)S(1)}, u32[]{:S(2)}, u32[]{:S(2)}) collective-permute-start(bf16[256,1024]{1,0:T(8,128)(2,1)S(1)} %get-tuple-element.11), channel_id=1, source_target_pairs={{28,0},{0,4},{4,8},{8,12},{12,16},{16,20},{20,24},{24,28},{29,1},{... | collective-permute-start | bytes 1572872 | tf_op jit(solution)/shard_map/ppermute | solution.py:13
  198.8 25.8 %collective-permute-start.5 = (bf16[256,1024]{1,0:T(8,128)(2,1)S(1)}, bf16[256,1024]{1,0:T(8,128)(2,1)S(1)}, u32[]{:S(2)}, u32[]{:S(2)}) collective-permute-start(bf16[256,1024]{1,0:T(8,128)(2,1)S(1)} %get-tuple-element.12), channel_id=1, source_target_pairs={{4,0},{8,4},{12,8},{16,12},{20,16},{24,20},{28,24},{0,28},{5,1},{9... | collective-permute-start | bytes 1572872 | tf_op jit(solution)/shard_map/ppermute | solution.py:13
  202.1 32.1 %collective-permute-start.4 = (bf16[256,1024]{1,0:T(8,128)(2,1)S(1)}, bf16[256,1024]{1,0:T(8,128)(2,1)S(1)}, u32[]{:S(2)}, u32[]{:S(2)}) collective-permute-start(bf16[256,1024]{1,0:T(8,128)(2,1)S(1)} %get-tuple-element.9), channel_id=1, source_target_pairs={{8,0},{12,4},{16,8},{20,12},{24,16},{28,20},{0,24},{4,28},{9,1},{1... | collective-permute-start | bytes 1572872 | tf_op jit(solution)/shard_map/ppermute | solution.py:13
Sparse Core Ops, SparseCore 0:
  52.7 100.5 all-gather.2
